TPU v7x, 32 devices: a whole 2x2x4 slice. The times are simulated.
32 devices in a mesh: cfg: 2 (over core), tm: 2 (over x), space: 8 (over z, y).
Axes of the slice: x: 2, y: 2, z: 4, core: 2. Of those that a mesh axis runs over, the one named last changes fastest.
Arguments:
- solutions: bfloat16 [4, 2, 3, 1024, 384], P(('cfg', 'tm'), None, None, 'space'), parts along dimension 0, may hold values from -6 to 6
- eigvecs: bfloat16 [4, 2, 3, 1024, 384], P(('cfg', 'tm'), None, None, 'space'), parts along dimension 0, may hold values from -0.078125 to 0.078125
- meson: bfloat16 [4, 4, 2, 384, 384], P(None, ('cfg', 'tm')), parts along dimension 1, may hold values from -0.015625 to 0.015625
- momenta: int32 [4, 3], replicated, may hold values from -3 to 3
- source_time: int32 [384], replicated, may hold values from 0 to 1
- dilution: int32 [384], replicated, may hold values from 0 to 3
Outputs:
- blocks: float32 [4, 2, 384, 4, 384], P(None, None, ('tm', 'space'), 'cfg'), parts along dimension 3
There are 2 independent parts, one for each index of `cfg`. A program takes and returns all parts, laid end to end along the dimension named above; an argument that names none is the same for every part. Nothing has to cross between parts.
All inputs are finite; a program needn't handle non-finite values.
Results may differ from a plain program's by a relative error of at most 0.0056.
Values may be sent and summed in bfloat16 or wider, within the bound.
A program may use at most 64 MiB of HBM per device.

v0:
```python
import jax
import jax.numpy as jnp
from jax import lax
from jax.sharding import PartitionSpec as P

SIDE = 48
NDIL = 4


def contract(first_op, second_op):
    return lax.dot_general(
        first_op, second_op, (((1,), (1,)), ((0,), (0,))), preferred_element_type=jnp.float32
    )


def regroup(array, time_count, space_count, cols_local):
    leading = array.shape[:-1]
    split = array.reshape(leading + (time_count, space_count, cols_local))
    return jnp.swapaxes(split, -3, -2).reshape(leading + (time_count * space_count * cols_local,))


def ungroup(array, time_count, space_count, cols_local):
    leading = array.shape[:-1]
    split = array.reshape(leading + (space_count, time_count, cols_local))
    return jnp.swapaxes(split, -3, -2).reshape(leading + (time_count * space_count * cols_local,))


def project(stack_real, stack_imag, vec_real, vec_imag, set_count, amount):
    real_part = contract(stack_real, vec_real) + contract(stack_imag, vec_imag)
    imag_part = contract(stack_imag, vec_real) - contract(stack_real, vec_imag)
    stacked = jnp.stack([real_part, imag_part], 2)
    times_local = stacked.shape[0]
    stacked = stacked.reshape(times_local, amount, set_count, 2, stacked.shape[-1])
    return jnp.transpose(stacked, (1, 0, 2, 3, 4))


def momentum_blocks(momentum, meson):
    coef_real = momentum[:, :, :, 0]
    coef_imag = momentum[:, :, :, 1]
    meson_real = meson[:, :, 0]
    meson_imag = meson[:, :, 1]
    left_real = jnp.einsum(
        "atpk,ptkl->ptal", coef_real, meson_real, preferred_element_type=jnp.float32
    ) + jnp.einsum("atpk,ptkl->ptal", coef_imag, meson_imag, preferred_element_type=jnp.float32)
    left_imag = jnp.einsum(
        "atpk,ptkl->ptal", coef_real, meson_imag, preferred_element_type=jnp.float32
    ) - jnp.einsum("atpk,ptkl->ptal", coef_imag, meson_real, preferred_element_type=jnp.float32)
    return (left_real.astype(jnp.bfloat16), left_imag.astype(jnp.bfloat16))


def meson_block(portion, patterns_all, left_real, left_imag):
    vectors = portion.shape[-1]
    dilution_mask = (
        (jnp.arange(vectors, dtype=jnp.int32) % NDIL)[None, :] == patterns_all[:, None]
    ).astype(jnp.bfloat16)
    zero_mom = portion * dilution_mask[:, None, None, :]
    zero_real = zero_mom[:, :, 0]
    zero_imag = zero_mom[:, :, 1]
    real_part = jnp.einsum(
        "ptal,btl->tapb", left_real, zero_real, preferred_element_type=jnp.float32
    ) - jnp.einsum("ptal,btl->tapb", left_imag, zero_imag, preferred_element_type=jnp.float32)
    imag_part = jnp.einsum(
        "ptal,btl->tapb", left_real, zero_imag, preferred_element_type=jnp.float32
    ) + jnp.einsum("ptal,btl->tapb", left_imag, zero_real, preferred_element_type=jnp.float32)
    return jnp.stack([real_part, imag_part], 3)


def body(solutions, eigvecs, meson, momenta, source_time, dilution):
    times_local, _, colors, sites_local, columns = solutions.shape
    vectors = eigvecs.shape[4]
    moments = momenta.shape[0]
    space_count = lax.axis_size("space")
    time_count = lax.axis_size("tm")
    rows_local = columns // space_count
    cols_local = columns // (space_count * time_count)
    times_total = times_local * time_count
    grouped = regroup(solutions, time_count, space_count, cols_local)
    patterns_all = regroup(dilution, time_count, space_count, cols_local)
    site_index = lax.axis_index("space") * sites_local + jnp.arange(sites_local, dtype=jnp.int32)
    coordinates = jnp.stack(
        [site_index % SIDE, site_index // SIDE % SIDE, site_index // (SIDE * SIDE)], 0
    )
    windings = jnp.sum(momenta[:, :, None] * coordinates[None], 1)
    angles = 2.0 * jnp.pi / SIDE * windings.astype(jnp.float32)
    cosine = jnp.cos(angles)[:, None, None, :, None]
    sine_part = jnp.sin(angles)[:, None, None, :, None]
    solve_real = grouped[:, 0].astype(jnp.float32)
    solve_imag = grouped[:, 1].astype(jnp.float32)
    phased_real = cosine * solve_real[None] + sine_part * solve_imag[None]
    phased_imag = cosine * solve_imag[None] - sine_part * solve_real[None]
    flat_rows = colors * sites_local
    phased_real = (
        jnp.moveaxis(phased_real, 0, -1)
        .reshape(times_local, flat_rows, columns * moments)
        .astype(jnp.bfloat16)
    )
    phased_imag = (
        jnp.moveaxis(phased_imag, 0, -1)
        .reshape(times_local, flat_rows, columns * moments)
        .astype(jnp.bfloat16)
    )
    base_real = grouped[:, 0].reshape(times_local, flat_rows, columns)
    base_imag = grouped[:, 1].reshape(times_local, flat_rows, columns)
    vec_real = eigvecs[:, 0].reshape(times_local, flat_rows, vectors)
    vec_imag = eigvecs[:, 1].reshape(times_local, flat_rows, vectors)
    zero_terms = project(base_real, base_imag, vec_real, vec_imag, 1, columns)
    zero_all = lax.psum(zero_terms, "space").astype(jnp.bfloat16)[:, :, 0]
    momentum = lax.psum_scatter(
        project(
            phased_real,
            phased_imag,
            vec_real,
            vec_imag,
            moments,
            rows_local * lax.axis_size("space"),
        ),
        "space",
        scatter_dimension=0,
        tiled=True,
    ).astype(jnp.bfloat16)
    left_real, left_imag = momentum_blocks(momentum, meson)
    blocks = meson_block(zero_all, patterns_all, left_real, left_imag)
    outgoing = blocks.reshape(times_local, time_count, cols_local, moments, 2, columns)
    first_row = (lax.axis_index("tm") * space_count + lax.axis_index("space")) * cols_local
    my_sources = lax.dynamic_slice_in_dim(source_time, first_row, cols_local)
    offsets = (
        my_sources[:, None] + jnp.arange(times_total, dtype=jnp.int32)[None, :]
    ) % times_total
    selector = (
        offsets[:, :, None] == jnp.arange(times_total, dtype=jnp.int32)[None, None, :]
    ).astype(jnp.float32)
    received = lax.all_to_all(
        outgoing.astype(jnp.bfloat16), "tm", split_axis=1, concat_axis=0, tiled=True
    ).astype(outgoing.dtype)
    by_time = received.reshape(times_total, cols_local, received.shape[3], 2, columns)
    by_time = ungroup(by_time, time_count, space_count, cols_local)
    return jnp.einsum("adt,taprb->pradb", selector, by_time, precision=lax.Precision.HIGHEST)


def solution(mesh):
    return jax.shard_map(
        body,
        mesh=mesh,
        in_specs=(
            P(("cfg", "tm"), None, None, "space", None),
            P(("cfg", "tm"), None, None, "space", None),
            P(None, ("cfg", "tm"), None, None, None),
            P(),
            P(),
            P(),
        ),
        out_specs=P(None, None, ("tm", "space"), "cfg", None),
        check_vma=False,
    )
```

profile of v0, /device:TPU:0, one launch (start us, length us, event | category | flops | bytes accessed | tf_op | source)
XLA Modules:
  0.0 181.8 jit_solution(11664704982364159849)
XLA Ops:
  6.5 0.0 reduce-scatter.2.cloned.1.call-start
  6.6 0.8 copy.53
  7.4 0.1 multiply_reduce_fusion
  7.5 1.4 copy.50
  8.9 0.1 copy.51
  8.9 0.0 copy-start.3
  8.9 0.1 fusion.46
  9.0 0.4 copy.54
  9.4 0.4 copy.55
  9.9 0.1 copy-done.3
  10.0 0.1 fusion.65
  10.1 0.0 copy-start.4
  10.1 1.7 add_convert_fusion
  11.8 0.9 fusion.8
  12.6 2.3 %fusion.4 = f32[1536,384]{1,0:T(8,128)} fusion(bf16[384,384]{1,0:T(8,128)(2,1)S(1)} %bitcast.165, bf16[192,8,3,128]{3,2,1,0:T(4,128)(2,1)S(1)} %bitcast.154), kind=kOutput, calls=%fused_computation.15 | convolution fusion | flops 452984832 | bytes 3833856 | tf_op jit(solution)/shard_map/dot_general | solution.py:11
  14.9 0.0 copy-done.4
  14.9 2.3 %convolution_add_fusion = f32[1536,384]{1,0:T(8,128)} fusion(f32[1536,384]{1,0:T(8,128)S(1)} %fusion.8, bf16[384,384]{1,0:T(8,128)(2,1)S(1)} %bitcast.162, bf16[192,8,3,128]{3,2,1,0:T(4,128)(2,1)S(1)} %bitcast.155), kind=kOutput, calls=%fused_computation.4 | convolution fusion | flops 453574656 | bytes 6193152 | tf_op jit(solution)/shard_map/dot_general | solution.py:11
  17.3 3.6 %stack.37 = f32[384,1,4,1,384]{4,2,0,3,1:T(4,128)} reshape(f32[1536,384]{1,0:T(8,128)} %convolution_add_fusion) | data formatting | bytes 4718592 | tf_op jit(solution)/shard_map/stack | solution.py:31
  20.8 0.0 copy-start
  20.9 0.0 copy-start.5
  20.9 3.4 %copy.56 = f32[384,1,4,1,384]{4,0,2,3,1:T(8,128)} copy(f32[384,1,4,1,384]{4,2,0,3,1:T(4,128)} %stack.37) | data formatting | bytes 4718592 | tf_op jit(solution)/shard_map/stack | solution.py:31
  24.2 0.0 copy-done
  24.2 0.0 copy-done.5
  24.2 2.3 %convolution_subtract_fusion = f32[1536,384]{1,0:T(8,128)} fusion(f32[1536,384]{1,0:T(8,128)S(1)} %copy-done, bf16[384,384]{1,0:T(8,128)(2,1)S(1)} %bitcast.163, bf16[192,8,3,128]{3,2,1,0:T(4,128)(2,1)S(1)} %bitcast.153), kind=kOutput, calls=%fused_computation.3 | convolution fusion | flops 453574656 | bytes 6193152 | tf_op jit(solution)/shard_map/dot_general | solution.py:11
  26.6 2.6 %stack.38 = f32[384,1,4,1,384]{4,2,0,3,1:T(4,128)S(1)} reshape(f32[1536,384]{1,0:T(8,128)} %convolution_subtract_fusion) | data formatting | bytes 4718592 | tf_op jit(solution)/shard_map/stack | solution.py:31
  29.2 0.0 copy-start.2
  29.2 0.2 copy.57
  29.4 1.5 copy-done.2
  30.9 2.4 %pad_maximum_fusion = f32[384,1,4,2,384]{4,0,2,3,1:T(8,128)} fusion(f32[384,1,4,1,384]{4,0,2,3,1:T(8,128)S(1)} %copy.57, f32[384,1,4,1,384]{4,0,2,3,1:T(8,128)S(1)} %copy-done.2), kind=kLoop, calls=%fused_computation | loop fusion | flops 1179648 | bytes 9437184 | tf_op jit(solution)/shard_map/stack | solution.py:31
  33.3 0.0 reduce-scatter.2.cloned.1.call-update
  33.3 0.3 convolution_bitcast_fusion.3
  33.7 0.3 convolution_bitcast_fusion.1
  34.0 0.3 fusion.1
  34.3 0.0 copy-start.6
  34.4 0.3 fusion.3
  34.7 0.1 maximum_bitcast_fusion
  34.8 0.2 copy-done.6
  35.0 0.0 copy-start.1
  35.0 0.1 reshape.419
  35.1 0.1 eq.40
  35.2 0.9 dynamic_slice.3
  36.1 0.9 compare_convert_fusion
  37.0 92.2 %all-reduce.1 = bf16[384,1,1,2,384]{4,0,3,2,1:T(8,128)(2,1)} all-reduce(f32[384,1,1,2,384]{4,0,3,2,1:T(8,128)S(1)} %maximum_bitcast_fusion), channel_id=1, replica_groups=mesh['cfg'=2,'tm'=2,'space'=8] {'space'}, use_global_device_ids=true, to_apply=%region_0.1 | all-reduce | flops 294912 | bytes 1769472 | tf_op jit(solution)/shard_map/psum | solution.py:107
  129.2 1.2 bitcast_multiply_fusion
  130.4 25.2 %reduce-scatter.2.cloned.1.call-done = f32[48,1,4,2,384]{4,0,2,3,1:T(8,128)} async-done(((f32[384,1,4,2,384]{4,0,2,3,1:T(8,128)}), f32[48,1,4,2,384]{4,0,2,3,1:T(8,128)}) %reduce-scatter.2.cloned.1.call-update) | async-done | bytes 589840 | tf_op jit(solution)/shard_map/reduce_scatter | solution.py:108
  155.6 1.1 convert_element_type.87
  156.7 0.0 copy-done.1
  156.7 0.3 fusion.12
  157.0 0.3 fusion.10
  157.3 0.3 fusion.29
  157.6 0.3 fusion.44
  157.9 0.3 fusion.45
  158.1 0.3 fusion.26
  158.4 0.3 fusion.24
  158.7 0.3 fusion.25
  159.0 0.7 copy.65
  159.8 3.6 %all-to-all-start = ((bf16[1,2,24,4,2,384]{5,2,3,4,0,1:T(8,128)(2,1)}), bf16[1,2,24,4,2,384]{5,2,3,4,0,1:T(8,128)(2,1)S(1)}, u32[]{:S(2)}, u32[]{:S(2)}) async-start(bf16[1,2,24,4,2,384]{5,2,3,4,0,1:T(8,128)(2,1)} %copy.65), calls=%async_computation.1 | async-start | bytes 589824 | tf_op jit(solution)/shard_map/all_to_all | solution.py:132
  163.4 0.1 add_select_fusion
  163.5 5.2 %all-to-all-done = bf16[1,2,24,4,2,384]{5,2,3,4,0,1:T(8,128)(2,1)S(1)} async-done(((bf16[1,2,24,4,2,384]{5,2,3,4,0,1:T(8,128)(2,1)}), bf16[1,2,24,4,2,384]{5,2,3,4,0,1:T(8,128)(2,1)S(1)}, u32[]{:S(2)}, u32[]{:S(2)}) %all-to-all-start) | async-done | bytes 294944 | tf_op jit(solution)/shard_map/all_to_all | solution.py:132
  168.7 2.0 %reshape_reshape.3 = bf16[2,24,4,2,8,2,24]{6,5,4,1,2,3,0:T(2,128)(2,1)S(1)} reshape(bf16[1,2,24,4,2,384]{5,2,3,4,0,1:T(8,128)(2,1)S(1)} %all-to-all-done) | data formatting | bytes 589824 | tf_op jit(solution)/shard_map/reshape;reshape | solution.py:24
  170.7 0.4 copy.87
  171.2 2.2 %reshape.428 = bf16[2,24,4,2,384]{4,0,3,2,1:T(2,128)(2,1)S(1)} reshape(bf16[2,24,4,2,2,8,24]{6,5,4,0,3,2,1:T(8,128)(2,1)S(1)} %bitcast.161) | data formatting | bytes 589824 | tf_op jit(solution)/shard_map/reshape | solution.py:25
  173.4 0.5 convolution_bitcast_fusion
  173.9 1.0 copy.63
  (7 shorter events, 0.1 us)
Async XLA Ops:
  6.5 149.1 %reduce-scatter.2.cloned.1.call-start = ((), (), s32[]{:S(2)}) async-start(), calls=%async_computation.2 | async-start | bytes 5308416 | tf_op jit(solution)/shard_map/reduce_scatter | solution.py:108
  8.9 1.1 copy-start.3
  10.1 4.9 %copy-start.4 = (bf16[1,1,3,128,384]{4,3,2,1,0:T(8,128)(2,1)}, bf16[1,1,3,128,384]{4,3,2,1,0:T(8,128)(2,1)S(1)}, u32[]{:S(2)}) copy-start(bf16[1,1,3,128,384]{4,3,2,1,0:T(8,128)(2,1)S(1)} %get-tuple-element.7) | copy-start | bytes 884740
  20.8 3.4 %copy-start = (f32[1536,384]{1,0:T(8,128)S(1)}, f32[1536,384]{1,0:T(8,128)}, u32[]{:S(2)}) copy-start(f32[1536,384]{1,0:T(8,128)} %fusion.4) | copy-start | bytes 7077892
  20.9 3.4 %copy-start.5 = (bf16[1,1,3,128,384]{4,3,2,1,0:T(8,128)(2,1)S(1)}, bf16[1,1,3,128,384]{4,3,2,1,0:T(8,128)(2,1)}, u32[]{:S(2)}) copy-start(bf16[1,1,3,128,384]{4,3,2,1,0:T(8,128)(2,1)} %copy-done.4) | copy-start | bytes 884740
  29.2 1.7 copy-start.2
  34.3 0.7 copy-start.6
  35.0 121.7 %copy-start.1 = (bf16[4,1,2,384,384]{4,3,2,1,0:T(8,128)(2,1)S(1)}, bf16[4,1,2,384,384]{4,3,2,1,0:T(8,128)(2,1)}, u32[]{:S(2)}) copy-start(bf16[4,1,2,384,384]{4,3,2,1,0:T(8,128)(2,1)} %param.8) | copy-start | bytes 7077892
  159.8 9.0 %all-to-all-start = ((bf16[1,2,24,4,2,384]{5,2,3,4,0,1:T(8,128)(2,1)}), bf16[1,2,24,4,2,384]{5,2,3,4,0,1:T(8,128)(2,1)S(1)}, u32[]{:S(2)}, u32[]{:S(2)}) async-start(bf16[1,2,24,4,2,384]{5,2,3,4,0,1:T(8,128)(2,1)} %copy.65), calls=%async_computation.1 | async-start | bytes 589824 | tf_op jit(solution)/shard_map/all_to_all | solution.py:132
Sparse Core Ops, SparseCore 0:
  33.4 122.1 reduce-scatter.1
where the time goes:
time: 182 us
  blocking collectives  92.2 us (51%)
  waiting for transfers between devices  30.5 us (17%)
  local copies, waits for them, and re-layouts  22.2 us (12%)
  between operations  13.7 us (8%)
  matrix products  11.9 us (7%)
  other arithmetic  7.73 us (4%)
  starting transfers between devices  3.63 us (2%)
    psum x1, blocking collectives, body(): zero_all = lax.psum(zero_terms, 'space').astype(jnp.bfloat16)[:, :, 0]  92.2 us
    reduce_scatter x1, waiting for transfers between devices, body(): lax.psum_scatter(project(phased_real, phased_imag, vec_real, vec_imag, mo...  25.2 us
    another operation x4, local copies, waits for them, and re-layouts, project(): stacked = jnp.stack([real_part, imag_part], 2)  9.73 us
    dot_general x8, matrix products, contract(): lax.dot_general(first_op, second_op, (((1,), (1,)), ((0,), (0,))), prefer...  9.17 us
    all_to_all x1, waiting for transfers between devices, body(): lax.all_to_all(outgoing.astype(jnp.bfloat16), 'tm', split_axis=1, concat_...  5.24 us
    unnamed x16, local copies, waits for them, and re-layouts  4.05 us
  transfers between devices with their start and end apart: 2, of which 2 were waited for; matrix products, arithmetic and copies ran while one was open for 3% of the time, Pallas kernels for 0%

commit v1 on v0

--- a/solution.py
+++ b/solution.py
@@ -1,3 +1,4 @@
+import functools
 import jax
 import jax.numpy as jnp
 from jax import lax
@@ -5,6 +6,15 @@
 
 SIDE = 48
 NDIL = 4
+
+
+def solve_wall_on_mesh(matrix, mesh_ax):
+    r1 = lax.all_gather(matrix, mesh_ax)
+    reply = jnp.sum(r1, axis=0)
+    return reply
+
+
+see_samples = functools.partial(solve_wall_on_mesh, mesh_ax="space")
 
 
 def contract(first_op, second_op):
@@ -104,7 +114,7 @@
     vec_real = eigvecs[:, 0].reshape(times_local, flat_rows, vectors)
     vec_imag = eigvecs[:, 1].reshape(times_local, flat_rows, vectors)
     zero_terms = project(base_real, base_imag, vec_real, vec_imag, 1, columns)
-    zero_all = lax.psum(zero_terms, "space").astype(jnp.bfloat16)[:, :, 0]
+    zero_all = see_samples(zero_terms).astype(jnp.bfloat16)[:, :, 0]
     momentum = lax.psum_scatter(
         project(
             phased_real,

time: 182 us -> 300 us (1.65)
  waiting for transfers between devices: 30.5 us -> 237 us
  blocking collectives: 92.2 us -> 0 us
  other arithmetic: 7.73 us -> 11.1 us
    all_gather x0 -> x1, waiting for transfers between devices: none -> 137 us  [solve_wall_on_mesh(): r1 = lax.all_gather(matrix, mesh_ax)]
    psum x1 -> x0, blocking collectives: 92.2 us -> none  [body(): zero_all = lax.psum(zero_terms, 'space').astype(jnp.bfloat16)[:, :, 0]]
    reduce_scatter x1, waiting for transfers between devices: 25.2 us -> 94.9 us  [body(): lax.psum_scatter(project(phased_real, phased_imag, vec_real, vec_imag, mo...]
    reduce_sum x0 -> x1, other arithmetic: none -> 4.19 us  [solve_wall_on_mesh(): reply = jnp.sum(r1, axis=0)]
  transfers between devices with their start and end apart: 2 -> 3, of which waited for: 2 -> 3; matrix products, arithmetic and copies ran while one was open for 3% -> 2% of each run, Pallas kernels for 0% -> 0%
where the time goes in v1:
time: 300 us; the launch traced here: 299 us
  waiting for transfers between devices  237 us (79%)
  local copies, waits for them, and re-layouts  21.8 us (7%)
  between operations  13.7 us (5%)
  matrix products  11.9 us (4%)
  other arithmetic  11.1 us (4%)
  starting transfers between devices  3.67 us (1%)
    all_gather x1, waiting for transfers between devices, solve_wall_on_mesh(): r1 = lax.all_gather(matrix, mesh_ax)  137 us
    reduce_scatter x1, waiting for transfers between devices, body(): lax.psum_scatter(project(phased_real, phased_imag, vec_real, vec_imag, mo...  94.9 us
    another operation x4, local copies, waits for them, and re-layouts, project(): stacked = jnp.stack([real_part, imag_part], 2)  9.7 us
    dot_general x8, matrix products, contract(): lax.dot_general(first_op, second_op, (((1,), (1,)), ((0,), (0,))), prefer...  9.14 us
  transfers between devices with their start and end apart: 3, of which 3 were waited for; matrix products, arithmetic and copies ran while one was open for 2% of the time, Pallas kernels for 0%

profile of v1, /device:TPU:0, one launch (start us, length us, event | category | flops | bytes accessed | tf_op | source)
XLA Modules:
  0.0 299.0 jit_solution(3352481038959387750)
XLA Ops:
  6.5 0.0 reduce-scatter.2.cloned.1.call-start
  6.6 0.8 copy.53
  7.4 0.1 multiply_reduce_fusion
  7.5 1.4 copy.50
  8.9 0.1 copy.51
  8.9 0.0 copy-start.3
  8.9 0.1 fusion.46
  9.0 0.4 copy.54
  9.4 0.4 copy.55
  9.9 0.1 copy-done.3
  10.0 0.1 fusion.65
  10.1 0.0 copy-start.4
  10.1 1.7 add_convert_fusion
  11.8 0.9 fusion.8
  12.6 2.3 fusion.4
  14.9 0.0 copy-done.4
  14.9 2.3 convolution_add_fusion
  17.2 3.6 %stack.37 = f32[384,1,4,1,384]{4,2,0,3,1:T(4,128)} reshape(f32[1536,384]{1,0:T(8,128)} %convolution_add_fusion) | data formatting | bytes 4718592 | tf_op jit(solution)/shard_map/stack | solution.py:41
  20.8 3.4 %copy.56 = f32[384,1,4,1,384]{4,0,2,3,1:T(8,128)} copy(f32[384,1,4,1,384]{4,2,0,3,1:T(4,128)} %stack.37) | data formatting | bytes 4718592 | tf_op jit(solution)/shard_map/stack | solution.py:41
  24.2 0.0 copy-done
  24.2 0.0 copy-done.5
  24.2 2.3 convolution_subtract_fusion
  26.5 2.6 stack.38
  29.1 0.0 copy-start.2
  29.1 0.2 copy.57
  29.3 1.5 copy-done.2
  30.8 2.5 pad_maximum_fusion
  33.3 0.0 reduce-scatter.2.cloned.1.call-update
  33.3 0.0 all-gather.3.cloned.1.call-start
  33.4 0.3 convolution_bitcast_fusion.3
  33.7 0.3 convolution_bitcast_fusion.1
  34.1 0.3 fusion.1
  34.4 0.0 copy-start.6
  34.4 0.3 fusion.3
  34.8 0.0 copy-start.1
  34.8 1.1 pad_maximum_fusion.1
  35.9 0.0 all-gather.3.cloned.1.call-update
  35.9 0.0 copy-done.6
  35.9 0.1 reshape.425
  36.0 0.1 eq.40
  36.1 0.8 dynamic_slice.3
  36.9 0.1 compare_convert_fusion
  37.0 94.9 %reduce-scatter.2.cloned.1.call-done = f32[48,1,4,2,384]{4,0,2,3,1:T(8,128)} async-done(((f32[384,1,4,2,384]{4,0,2,3,1:T(8,128)}), f32[48,1,4,2,384]{4,0,2,3,1:T(8,128)}) %reduce-scatter.2.cloned.1.call-update) | async-done | bytes 589840 | tf_op jit(solution)/shard_map/reduce_scatter | solution.py:118
  131.9 1.1 convert_element_type.101
  133.0 0.3 fusion.12
  133.3 0.3 fusion.10
  133.6 0.3 fusion.29
  133.9 0.3 fusion.26
  134.2 136.8 %all-gather.3.cloned.1.call-done = f32[8,384,2,384]{3,1,2,0:T(8,128)} async-done(((f32[1,384,2,384]{3,1,2,0:T(8,128)}), f32[8,384,2,384]{3,1,2,0:T(8,128)}) %all-gather.3.cloned.1.call-update) | async-done | bytes 9437200 | tf_op jit(solution)/shard_map/all_gather | solution.py:12
  271.0 4.2 %reduce.1 = bf16[384,2,384]{2,0,1:T(8,128)(2,1)S(1)} reduce(f32[8,384,2,384]{3,1,2,0:T(8,128)} %all-gather.3.cloned.1.call-done, f32[]{:T(128)} %constant.62.clone.1), dimensions={0}, to_apply=%region_0.1 | reduce | flops 2064384 | bytes 10027012 | tf_op jit(solution)/shard_map/reduce_sum | solution.py:13
  275.2 0.1 bitcast_multiply_fusion
  275.3 0.3 fusion.44
  275.5 0.3 fusion.45
  275.8 0.3 fusion.24
  276.1 0.3 fusion.25
  276.4 0.7 copy.65
  277.1 3.6 %all-to-all-start = ((bf16[1,2,24,4,2,384]{5,2,3,4,0,1:T(8,128)(2,1)}), bf16[1,2,24,4,2,384]{5,2,3,4,0,1:T(8,128)(2,1)S(1)}, u32[]{:S(2)}, u32[]{:S(2)}) async-start(bf16[1,2,24,4,2,384]{5,2,3,4,0,1:T(8,128)(2,1)} %copy.65), calls=%async_computation.1 | async-start | bytes 589824 | tf_op jit(solution)/shard_map/all_to_all | solution.py:142
  280.8 0.1 add_select_fusion
  280.9 5.1 %all-to-all-done = bf16[1,2,24,4,2,384]{5,2,3,4,0,1:T(8,128)(2,1)S(1)} async-done(((bf16[1,2,24,4,2,384]{5,2,3,4,0,1:T(8,128)(2,1)}), bf16[1,2,24,4,2,384]{5,2,3,4,0,1:T(8,128)(2,1)S(1)}, u32[]{:S(2)}, u32[]{:S(2)}) %all-to-all-start) | async-done | bytes 294944 | tf_op jit(solution)/shard_map/all_to_all | solution.py:142
  285.9 2.0 reshape_reshape.3
  288.0 0.4 copy.87
  288.4 2.2 reshape.434
  290.6 0.5 convolution_bitcast_fusion
  291.1 1.0 copy.63
  (10 shorter events, 0.1 us)
Async XLA Ops:
  6.5 125.4 %reduce-scatter.2.cloned.1.call-start = ((), (), s32[]{:S(2)}) async-start(), calls=%async_computation.2 | async-start | bytes 5308416 | tf_op jit(solution)/shard_map/reduce_scatter | solution.py:118
  8.9 1.1 copy-start.3
  10.1 4.9 %copy-start.4 = (bf16[1,1,3,128,384]{4,3,2,1,0:T(8,128)(2,1)}, bf16[1,1,3,128,384]{4,3,2,1,0:T(8,128)(2,1)S(1)}, u32[]{:S(2)}) copy-start(bf16[1,1,3,128,384]{4,3,2,1,0:T(8,128)(2,1)S(1)} %get-tuple-element.7) | copy-start | bytes 884740
  20.8 3.4 %copy-start = (f32[1536,384]{1,0:T(8,128)S(1)}, f32[1536,384]{1,0:T(8,128)}, u32[]{:S(2)}) copy-start(f32[1536,384]{1,0:T(8,128)} %fusion.4) | copy-start | bytes 7077892
  20.8 3.4 %copy-start.5 = (bf16[1,1,3,128,384]{4,3,2,1,0:T(8,128)(2,1)S(1)}, bf16[1,1,3,128,384]{4,3,2,1,0:T(8,128)(2,1)}, u32[]{:S(2)}) copy-start(bf16[1,1,3,128,384]{4,3,2,1,0:T(8,128)(2,1)} %copy-done.4) | copy-start | bytes 884740
  29.1 1.7 copy-start.2
  33.3 237.7 %all-gather.3.cloned.1.call-start = ((), (), s32[]{:S(2)}) async-start(), calls=%async_computation.3 | async-start | bytes 10616832 | tf_op jit(solution)/shard_map/all_gather | solution.py:12
  34.4 1.5 copy-start.6
  34.8 98.2 %copy-start.1 = (bf16[4,1,2,384,384]{4,3,2,1,0:T(8,128)(2,1)S(1)}, bf16[4,1,2,384,384]{4,3,2,1,0:T(8,128)(2,1)}, u32[]{:S(2)}) copy-start(bf16[4,1,2,384,384]{4,3,2,1,0:T(8,128)(2,1)} %param.8) | copy-start | bytes 7077892
  277.1 8.8 %all-to-all-start = ((bf16[1,2,24,4,2,384]{5,2,3,4,0,1:T(8,128)(2,1)}), bf16[1,2,24,4,2,384]{5,2,3,4,0,1:T(8,128)(2,1)S(1)}, u32[]{:S(2)}, u32[]{:S(2)}) async-start(bf16[1,2,24,4,2,384]{5,2,3,4,0,1:T(8,128)(2,1)} %copy.65), calls=%async_computation.1 | async-start | bytes 589824 | tf_op jit(solution)/shard_map/all_to_all | solution.py:142
Sparse Core Ops, SparseCore 0:
  33.5 98.3 reduce-scatter.1
  134.1 136.8 all-gather.2
